TPU v7x, 512 devices: a whole 4x8x8 slice. The times are simulated.
512 devices in a mesh: slab: 128 (over y, z, core), case: 4 (over x).
Axes of the slice: x: 4, y: 8, z: 8, core: 2. Of those that a mesh axis runs over, the one named last changes fastest.
Arguments:
- pressure: float32 [64, 512], replicated, may hold values from -9 to 9
- panel: int32 [1536, 4, 128], P('slab'), may hold values from 0 to 511
- flags: int32 [1536, 4, 128], P('slab'), may hold values 0 or 1
- diagonal: float32 [1536, 4, 128], P('slab'), may hold values from 0.25 to 4
Outputs:
- fields: float32 [64, 1536, 4, 128], P('case', 'slab')
- gram: float32 [64, 64], P('case')
- cross: float32 [64, 64], P('case')
All inputs are finite; a program needn't handle non-finite values. No bound on the sum of `flags` on one device may be relied on, other than what follows from the above.
Results may differ from a plain program's by a relative error of at most 0.00005.
Values sent between devices are 32-bit elements; how exact they have to be, the bound alone decides.
A program may use at most 64 MiB of HBM per device.

v0:
```python
import jax
import jax.numpy as jnp
from jax import lax
from jax.sharding import PartitionSpec as P

damping = 0.7
penalty = 4.0
highest = lax.Precision.HIGHEST


def with_halo(cells, sides, width):
    for axis, dim in sides:
        count = lax.axis_size(axis)
        ends = count - 1
        head = lax.slice_in_dim(cells, 0, width, axis=dim)
        tail = lax.slice_in_dim(cells, cells.shape[dim] - width, cells.shape[dim], axis=dim)
        cells = jnp.concatenate(
            [
                lax.ppermute(tail, axis, [(i, (i + 1) % count) for i in range(ends)]),
                cells,
                lax.ppermute(head, axis, [((i + 1) % count, i) for i in range(ends)]),
            ],
            axis=dim,
        )
    return cells


def from_behind(x, axis, by):
    count = lax.axis_size(axis)
    pairs = [(i, i + by) for i in range(count) if 0 <= i + by < count]
    return lax.ppermute(x, axis, pairs)


def transverse(field):
    beside_all = jnp.roll(field, 1, axis=-1) + jnp.roll(field, -1, axis=-1)
    zero_row = jnp.zeros_like(field[..., :1, :])
    inward = jnp.concatenate([zero_row, field[..., :-1, :]], axis=-2)
    outward = jnp.concatenate([field[..., 1:, :], zero_row], axis=-2)
    return beside_all + inward + outward


def stencil(field, below, above, coeff, weight):
    return (coeff + 2.0 * weight + 4.0) * field - weight * (below + above) - transverse(field)


def apply_halo(field, coeff, weight):
    padded = with_halo(field, (("slab", 1),), 1)
    return stencil(field, padded[:, :-2], padded[:, 2:], coeff, weight)


def smooth_halo(field, rhs, coeff, weight):
    return field + damping * (rhs - apply_halo(field, coeff, weight)) / (coeff + 2.0 * weight + 4.0)


def restrict(fine):
    even = fine[:, 0::2]
    odd = fine[:, 1::2]
    lower = from_behind(fine[:, -1:], "slab", 1)
    odd_before = jnp.concatenate([lower, odd[:, :-1]], axis=1)
    return 0.5 * even + 0.25 * (odd + odd_before)


def prolong(coarse):
    upper = from_behind(coarse[:, :1], "slab", -1)
    following = jnp.concatenate([coarse[:, 1:], upper], axis=1)
    middle = 0.5 * (coarse + following)
    stacked = jnp.stack([coarse, middle], axis=2)
    shape = coarse.shape
    return stacked.reshape(shape[0], 2 * shape[1], shape[2], shape[3])


def coarsest(rhs, coeff, weight):
    field = damping * rhs / (coeff + 2.0 * weight + 4.0)
    for sweep in range(3):
        field = smooth_halo(field, rhs, coeff, weight)
    return field


def vcycle(rhs, coeff, level):
    weight = 0.25**level
    if level == 2:
        return coarsest(rhs, coeff, weight)
    field = damping * rhs / (coeff + 2.0 * weight + 4.0)
    field = smooth_halo(field, rhs, coeff, weight)
    leftover = rhs - apply_halo(field, coeff, weight)
    coarse_coeff = 0.5 * (coeff[0::2] + coeff[1::2])
    field = field + prolong(vcycle(restrict(leftover), coarse_coeff, level + 1))
    for sweep in range(2):
        field = smooth_halo(field, rhs, coeff, weight)
    return field


def local(pressure, panel, flags, diagonal):
    layers, radial, beside_all = panel.shape
    slabs = lax.axis_size("slab")
    groups = lax.axis_size("case")
    per_group = pressure.shape[0] // groups
    total_layers = layers * slabs
    own_group = lax.axis_index("case")
    case_rows = lax.dynamic_slice_in_dim(pressure, own_group * per_group, per_group, 0)
    coeff = diagonal + penalty * flags.astype(jnp.float32)
    keep = 1.0 - flags.astype(jnp.float32)
    positions = (lax.axis_index("slab") * layers + jnp.arange(layers)).astype(jnp.float32)
    span = (1.0 + 2.0 * positions / total_layers)[:, None, None]
    loads = jnp.take(case_rows, panel, axis=1) * span * keep
    fields = vcycle(loads, coeff, 0)
    images = apply_halo(fields, coeff, 1.0)
    scale = 1.0 / (total_layers * radial * beside_all)
    contract = (((1,), (1,)), ((), ()))
    images_flat = images.reshape(per_group, -1)
    loads_flat = loads.reshape(per_group, -1)
    piece = lax.all_gather(fields, "case", axis=0, tiled=True)
    piece_flat = piece.reshape(piece.shape[0], -1)
    gram_block = lax.dot_general(
        images_flat, piece_flat, contract, precision=highest, preferred_element_type=jnp.float32
    )
    cross_block = lax.dot_general(
        loads_flat, piece_flat, contract, precision=highest, preferred_element_type=jnp.float32
    )
    gram_rows, cross_rows = lax.psum((gram_block, cross_block), "slab")
    return (fields, gram_rows * scale, cross_rows * scale)


def solution(mesh):
    in_specs = (P(), P("slab", None, None), P("slab", None, None), P("slab", None, None))
    out_specs = (P("case", "slab", None, None), P("case", None), P("case", None))
    return jax.shard_map(local, mesh=mesh, in_specs=in_specs, out_specs=out_specs, check_vma=False)
```

profile of v0, /device:TPU:2, one launch (start us, length us, event | category | flops | bytes accessed | tf_op | source)
XLA Modules:
  0.0 730.1 jit_solution(7467663255318855311)
XLA Ops:
  8.9 20.9 %gather_fusion = f32[6144,16]{1,0:T(8,128)} fusion(f32[16,512]{0,1:T(8,128)S(1)} %copy.21, s32[6144]{0:T(1024)S(1)} %broadcast_clamp_fusion), kind=kCustom, calls=%fused_computation | custom fusion | bytes 811008 | tf_op jit(solution)/shard_map/jit(_take)/gather | solution.py:105
  29.9 2.3 copy.13
  32.4 1.7 collective-permute-start
  34.2 1.3 collective-permute-start.1
  35.9 3.5 collective-permute-done.1
  40.3 4.5 collective-permute-start.2
  44.8 1.3 collective-permute-start.3
  46.2 1.7 collective-permute-done.3
  48.4 4.8 collective-permute-start.4
  54.3 2.3 collective-permute-start.5
  56.6 1.3 collective-permute-start.6
  57.9 3.4 collective-permute-done.6
  61.8 4.5 collective-permute-start.7
  66.3 1.3 collective-permute-start.8
  67.6 3.5 collective-permute-done.8
  71.4 5.4 collective-permute-start.9
  77.9 2.3 collective-permute-start.10
  80.2 1.3 collective-permute-start.11
  81.5 3.9 collective-permute-done.11
  85.7 4.5 collective-permute-start.12
  90.3 1.3 collective-permute-start.13
  91.6 3.6 collective-permute-done.13
  95.5 5.4 collective-permute-start.14
  100.9 1.3 collective-permute-start.15
  102.3 1.8 collective-permute-done.15
  104.2 1.3 collective-permute-start.16
  105.5 4.6 collective-permute-done.16
  110.5 4.5 collective-permute-start.17
  115.0 1.3 collective-permute-start.18
  116.4 3.5 collective-permute-done.18
  120.4 5.4 collective-permute-start.19
  125.8 1.3 collective-permute-start.20
  127.1 1.8 collective-permute-done.20
  129.1 1.3 collective-permute-start.21
  130.4 4.6 collective-permute-done.21
  135.6 4.5 collective-permute-start.22
  140.2 1.3 collective-permute-start.23
  141.5 2.8 collective-permute-done.23
  145.2 5.4 collective-permute-start.24
  150.6 1.3 collective-permute-start.25
  152.0 1.7 collective-permute-done.25
  155.0 1.9 copy.16
  157.7 5.3 collective-permute-start.26
  162.9 1.3 collective-permute-start.27
  164.7 57.1 %all-gather.2.cloned.1.call-done = f32[64,12,4,128]{3,0,2,1:T(8,128)} async-done(((f32[16,12,4,128]{3,0,2,1:T(8,128)}), f32[64,12,4,128]{3,0,2,1:T(8,128)}) %all-gather.2.cloned.1.call-update) | async-done | bytes 1572880 | tf_op jit(solution)/shard_map/all_gather | solution.py:112
  221.8 2.9 convolution_bitcast_fusion
  224.7 1.4 convolution_bitcast_fusion.1
  226.2 496.5 %all-reduce.24 = (f32[16,64]{1,0:T(8,128)S(1)}, f32[16,64]{1,0:T(8,128)S(1)}) all-reduce(f32[16,64]{1,0:T(8,128)S(1)} %convolution_bitcast_fusion.1, f32[16,64]{1,0:T(8,128)S(1)} %convolution_bitcast_fusion), channel_id=1, replica_groups=mesh['slab'=128,'case'=4] {'slab'}, use_global_device_ids=true, to_apply=%region_0.1 | all-reduce | flops 2048 | bytes 16384 | tf_op jit(solution)/shard_map/psum | solution.py:120
  (117 shorter events, 12.7 us)
Async XLA Ops:
  7.2 1.6 copy-start
  7.2 214.6 %all-gather.2.cloned.1.call-start = ((), (), s32[]{:S(2)}) async-start(), calls=%async_computation | async-start | bytes 1966080 | tf_op jit(solution)/shard_map/all_gather | solution.py:112
  29.9 2.3 copy-start.3
  29.9 2.4 copy-start.4
  32.4 3.5 collective-permute-start
  34.2 5.3 collective-permute-start.1
  40.3 5.9 collective-permute-start.2
  44.8 3.1 collective-permute-start.3
  48.4 5.6 collective-permute-start.4
  54.3 3.6 collective-permute-start.5
  56.6 4.8 collective-permute-start.6
  61.8 5.9 collective-permute-start.7
  66.3 4.9 collective-permute-start.8
  71.4 6.3 collective-permute-start.9
  77.9 3.6 collective-permute-start.10
  80.2 5.2 collective-permute-start.11
  85.7 5.9 collective-permute-start.12
  90.3 4.9 collective-permute-start.13
  95.5 6.8 collective-permute-start.14
  100.9 3.1 collective-permute-start.15
  104.2 6.0 collective-permute-start.16
  110.5 5.9 collective-permute-start.17
  115.0 4.9 collective-permute-start.18
  120.4 6.8 collective-permute-start.19
  125.8 3.1 collective-permute-start.20
  129.1 6.0 collective-permute-start.21
  135.6 5.9 collective-permute-start.22
  140.2 4.1 collective-permute-start.23
  145.2 6.8 collective-permute-start.24
  150.6 3.1 collective-permute-start.25
  154.9 9.3 %copy-start.1 = (f32[16,12,4,128]{3,0,2,1:T(8,128)S(1)}, f32[16,12,4,128]{3,0,2,1:T(8,128)}, u32[]{:S(2)}) copy-start(f32[16,12,4,128]{3,0,2,1:T(8,128)} %fusion.12) | copy-start | bytes 1179652
  157.7 67.0 %collective-permute-start.26 = (f32[16,1,4,128]{3,0,2,1:T(8,128)S(1)}, f32[16,1,4,128]{3,0,2,1:T(8,128)S(1)}, u32[]{:S(2)}, u32[]{:S(2)}) collective-permute-start(f32[16,1,4,128]{3,0,2,1:T(8,128)S(1)} %get-tuple-element.25), channel_id=1, source_target_pairs={{0,4},{4,8},{8,12},{12,16},{16,20},{20,24},{24,28},{28,32},{32,36}... | collective-permute-start | bytes 98312 | tf_op jit(solution)/shard_map/ppermute | solution.py:19
  162.9 61.8 %collective-permute-start.27 = (f32[16,1,4,128]{3,0,2,1:T(8,128)S(1)}, f32[16,1,4,128]{3,0,2,1:T(8,128)S(1)}, u32[]{:S(2)}, u32[]{:S(2)}) collective-permute-start(f32[16,1,4,128]{3,0,2,1:T(8,128)S(1)} %get-tuple-element.26), channel_id=1, source_target_pairs={{4,0},{8,4},{12,8},{16,12},{20,16},{24,20},{28,24},{32,28},{36,32}... | collective-permute-start | bytes 98312 | tf_op jit(solution)/shard_map/ppermute | solution.py:21
  221.8 2.9 copy-start.2
Sparse Core Ops, SparseCore 0:
  155.1 66.6 all-gather.1
where the time goes:
time: 731 us; the launch traced here: 730 us
  blocking collectives  497 us (68%)
  waiting for transfers between devices  99.3 us (14%)
  starting transfers between devices  78.8 us (11%)
  local copies, waits for them, and re-layouts  29.9 us (4%)
  between operations  14.9 us (2%)
    psum x1, blocking collectives, local(): gram_rows, cross_rows = lax.psum((gram_block, cross_block), 'slab')  497 us
    all_gather x1, waiting for transfers between devices, local(): piece = lax.all_gather(fields, 'case', axis=0, tiled=True)  57.1 us
    ppermute x12, starting transfers between devices, with_halo(): lax.ppermute(tail, axis, [(i, (i + 1) % count) for i in range(ends)])  50.5 us
    ppermute x12, waiting for transfers between devices, with_halo(): lax.ppermute(head, axis, [((i + 1) % count, i) for i in range(ends)])  31.3 us
    gather x2, local copies, waits for them, and re-layouts, local(): loads = jnp.take(case_rows, panel, axis=1) * span * keep  23.3 us
    ppermute x12, starting transfers between devices, with_halo(): lax.ppermute(head, axis, [((i + 1) % count, i) for i in range(ends)])  15.5 us
  transfers between devices with their start and end apart: 29, of which 16 were waited for; matrix products, arithmetic and copies ran while one was open for 1% of the time, Pallas kernels for 0%

commit v1 on v0

--- a/solution.py
+++ b/solution.py
@@ -6,6 +6,12 @@
 damping = 0.7
 penalty = 4.0
 highest = lax.Precision.HIGHEST
+
+
+def joined_along(pieces, dim):
+    pieces = jnp.moveaxis(pieces, 0, dim)
+    shape = pieces.shape
+    return pieces.reshape(*shape[:dim], shape[dim] * shape[dim + 1], *shape[dim + 2 :])
 
 
 def with_halo(cells, sides, width):
@@ -109,7 +115,19 @@
     contract = (((1,), (1,)), ((), ()))
     images_flat = images.reshape(per_group, -1)
     loads_flat = loads.reshape(per_group, -1)
-    piece = lax.all_gather(fields, "case", axis=0, tiled=True)
+    devices = lax.axis_size("case")
+    pairs_2 = [(i_2, (i_2 + 1) % devices) for i_2 in range(devices)]
+    back = [(b, a) for a, b in pairs_2]
+    lower_2, upper_2 = ([], [])
+    for step in range(devices - 1):
+        if step % 2 == 0:
+            lower_2.append(lax.ppermute(lower_2[-1] if lower_2 else fields, "case", pairs_2))
+        else:
+            upper_2.append(lax.ppermute(upper_2[-1] if upper_2 else fields, "case", back))
+    parts = jnp.stack([*lower_2[::-1], fields, *upper_2])
+    shift = lax.axis_index("case") - len(lower_2)
+    parts = parts[(jnp.arange(devices) - shift) % devices]
+    piece = joined_along(parts, 0)
     piece_flat = piece.reshape(piece.shape[0], -1)
     gram_block = lax.dot_general(
         images_flat, piece_flat, contract, precision=highest, preferred_element_type=jnp.float32

time: 731 us -> 722 us (0.988)
  the two profiles are of different devices: /device:TPU:2 before, /device:TPU:32 now
where the time goes in v1:
time: 722 us; the launch traced here: 721 us
  blocking collectives  491 us (68%)
  waiting for transfers between devices  95.1 us (13%)
  starting transfers between devices  85.3 us (12%)
  local copies, waits for them, and re-layouts  34.8 us (5%)
  other arithmetic  10.6 us (1%)
    psum x1, blocking collectives, local(): gram_rows, cross_rows = lax.psum((gram_block, cross_block), 'slab')  491 us
    ppermute x12, waiting for transfers between devices, with_halo(): lax.ppermute(tail, axis, [(i, (i + 1) % count) for i in range(ends)])  67 us
    ppermute x12, starting transfers between devices, with_halo(): lax.ppermute(head, axis, [((i + 1) % count, i) for i in range(ends)])  41.5 us
    ppermute x12, starting transfers between devices, with_halo(): lax.ppermute(tail, axis, [(i, (i + 1) % count) for i in range(ends)])  27.6 us
    gather x2, local copies, waits for them, and re-layouts, local(): loads = jnp.take(case_rows, panel, axis=1) * span * keep  23.3 us
    ppermute x4, waiting for transfers between devices, from_behind(): return lax.ppermute(x, axis, pairs)  16 us
  transfers between devices with their start and end apart: 31, of which 17 were waited for; matrix products, arithmetic and copies ran while one was open for 0% of the time, Pallas kernels for 0%

profile of v1, /device:TPU:32, one launch (start us, length us, event | category | flops | bytes accessed | tf_op | source)
XLA Modules:
  0.0 720.9 jit_solution(17344483461186472931)
XLA Ops:
  2.4 21.0 %gather_fusion = f32[6144,16]{1,0:T(8,128)} fusion(f32[16,512]{0,1:T(8,128)S(1)} %copy.11, s32[6144]{0:T(1024)S(1)} %broadcast_clamp_fusion), kind=kCustom, calls=%fused_computation | custom fusion | bytes 811008 | tf_op jit(solution)/shard_map/jit(_take)/gather | solution.py:111
  23.4 2.3 copy.8
  26.0 10.3 %collective-permute-start.1 = (f32[16,1,4,128]{3,2,1,0:T(4,128)S(1)}, f32[16,1,4,128]{3,2,1,0:T(4,128)S(1)}, u32[]{:S(2)}, u32[]{:S(2)}) collective-permute-start(f32[16,1,4,128]{3,2,1,0:T(4,128)S(1)} %get-tuple-element.54), channel_id=1, source_target_pairs={{4,0},{8,4},{12,8},{16,12},{20,16},{24,20},{28,24},{32,28},{36,32}... | collective-permute-start | bytes 98312 | tf_op jit(solution)/shard_map/ppermute | solution.py:27
  36.3 1.9 collective-permute-start
  38.9 5.9 collective-permute-done
  48.1 2.4 collective-permute-start.2
  50.7 6.0 collective-permute-done.2
  57.4 1.9 collective-permute-start.4
  59.4 6.5 collective-permute-done.4
  66.5 1.9 collective-permute-start.6
  68.4 2.4 collective-permute-start.5
  70.9 6.0 collective-permute-done.5
  77.8 1.9 collective-permute-start.8
  79.7 2.4 collective-permute-start.7
  82.2 6.0 collective-permute-done.7
  88.7 1.9 collective-permute-start.9
  90.6 6.6 collective-permute-done.9
  97.5 1.9 collective-permute-start.11
  99.5 2.4 collective-permute-start.10
  101.9 6.1 collective-permute-done.10
  108.5 1.9 collective-permute-start.13
  110.4 2.4 collective-permute-start.12
  112.9 6.1 collective-permute-done.12
  119.5 1.9 collective-permute-start.15
  121.4 2.4 collective-permute-start.14
  123.9 6.1 collective-permute-done.14
  130.2 1.9 collective-permute-start.16
  134.3 7.0 collective-permute-start.18
  141.2 1.9 collective-permute-start.17
  143.3 6.5 collective-permute-done.17
  150.6 1.9 collective-permute-start.20
  152.5 2.4 collective-permute-start.19
  155.0 6.0 collective-permute-done.19
  161.5 1.9 collective-permute-start.21
  165.9 7.0 collective-permute-start.23
  172.9 2.1 collective-permute-start.22
  175.2 6.3 collective-permute-done.22
  184.7 2.4 collective-permute-start.24
  187.3 6.0 collective-permute-done.24
  194.1 4.7 collective-permute-start.30
  198.8 1.9 collective-permute-start.28
  200.7 1.9 collective-permute-start.27
  202.7 2.4 collective-permute-start.26
  205.6 4.1 collective-permute-done.28
  212.7 8.0 %collective-permute-done.29 = f32[16,12,4,128]{3,2,1,0:T(4,128)} collective-permute-done((f32[16,12,4,128]{3,2,1,0:T(4,128)S(1)}, f32[16,12,4,128]{3,2,1,0:T(4,128)}, u32[]{:S(2)}, u32[]{:S(2)}) %collective-permute-start.29) | collective-permute-done | bytes 393248 | tf_op jit(solution)/shard_map/ppermute | solution.py:124
  222.2 2.5 gather_fusion.1
  224.7 2.0 reshape_reshape.3
  229.4 491.0 %all-reduce.24 = (f32[16,64]{1,0:T(8,128)S(1)}, f32[16,64]{1,0:T(8,128)S(1)}) all-reduce(f32[16,64]{1,0:T(8,128)S(1)} %fusion.147, f32[16,64]{1,0:T(8,128)S(1)} %fusion.148), channel_id=1, replica_groups=mesh['slab'=128,'case'=4] {'slab'}, use_global_device_ids=true, to_apply=%region_0.1 | all-reduce | flops 2048 | bytes 16384 | tf_op jit(solution)/shard_map/psum | solution.py:138
  (127 shorter events, 28.8 us)
Async XLA Ops:
  0.6 1.6 copy-start
  23.4 2.4 copy-start.3
  23.4 2.4 copy-start.4
  26.0 12.9 %collective-permute-start.1 = (f32[16,1,4,128]{3,2,1,0:T(4,128)S(1)}, f32[16,1,4,128]{3,2,1,0:T(4,128)S(1)}, u32[]{:S(2)}, u32[]{:S(2)}) collective-permute-start(f32[16,1,4,128]{3,2,1,0:T(4,128)S(1)} %get-tuple-element.54), channel_id=1, source_target_pairs={{4,0},{8,4},{12,8},{16,12},{20,16},{24,20},{28,24},{32,28},{36,32}... | collective-permute-start | bytes 98312 | tf_op jit(solution)/shard_map/ppermute | solution.py:27
  36.3 8.6 %collective-permute-start = (f32[16,1,4,128]{3,2,1,0:T(4,128)S(1)}, f32[16,1,4,128]{3,2,1,0:T(4,128)S(1)}, u32[]{:S(2)}, u32[]{:S(2)}) collective-permute-start(f32[16,1,4,128]{3,2,1,0:T(4,128)S(1)} %get-tuple-element.53), channel_id=1, source_target_pairs={{0,4},{4,8},{8,12},{12,16},{16,20},{20,24},{24,28},{28,32},{32,36}... | collective-permute-start | bytes 98312 | tf_op jit(solution)/shard_map/ppermute | solution.py:25
  46.2 4.5 collective-permute-start.3
  48.1 8.6 %collective-permute-start.2 = (f32[16,1,4,128]{3,2,1,0:T(4,128)S(1)}, f32[16,1,4,128]{3,2,1,0:T(4,128)S(1)}, u32[]{:S(2)}, u32[]{:S(2)}) collective-permute-start(f32[16,1,4,128]{3,2,1,0:T(4,128)S(1)} %get-tuple-element.45), channel_id=1, source_target_pairs={{0,4},{4,8},{8,12},{12,16},{16,20},{20,24},{24,28},{28,32},{32,36}... | collective-permute-start | bytes 98312 | tf_op jit(solution)/shard_map/ppermute | solution.py:25
  57.4 8.6 %collective-permute-start.4 = (f32[16,1,4,128]{3,2,1,0:T(4,128)S(1)}, f32[16,1,4,128]{3,2,1,0:T(4,128)S(1)}, u32[]{:S(2)}, u32[]{:S(2)}) collective-permute-start(f32[16,1,4,128]{3,2,1,0:T(4,128)S(1)} %slice.600), channel_id=1, source_target_pairs={{0,4},{4,8},{8,12},{12,16},{16,20},{20,24},{24,28},{28,32},{32,36}... | collective-permute-start | bytes 98312 | tf_op jit(solution)/shard_map/ppermute | solution.py:37
  66.5 4.4 collective-permute-start.6
  68.4 8.6 %collective-permute-start.5 = (f32[16,1,4,128]{3,2,1,0:T(4,128)S(1)}, f32[16,1,4,128]{3,2,1,0:T(4,128)S(1)}, u32[]{:S(2)}, u32[]{:S(2)}) collective-permute-start(f32[16,1,4,128]{3,2,1,0:T(4,128)S(1)} %get-tuple-element.85), channel_id=1, source_target_pairs={{0,4},{4,8},{8,12},{12,16},{16,20},{20,24},{24,28},{28,32},{32,36}... | collective-permute-start | bytes 98312 | tf_op jit(solution)/shard_map/ppermute | solution.py:25
  77.8 4.4 collective-permute-start.8
  79.7 8.6 %collective-permute-start.7 = (f32[16,1,4,128]{3,2,1,0:T(4,128)S(1)}, f32[16,1,4,128]{3,2,1,0:T(4,128)S(1)}, u32[]{:S(2)}, u32[]{:S(2)}) collective-permute-start(f32[16,1,4,128]{3,2,1,0:T(4,128)S(1)} %get-tuple-element.77), channel_id=1, source_target_pairs={{0,4},{4,8},{8,12},{12,16},{16,20},{20,24},{24,28},{28,32},{32,36}... | collective-permute-start | bytes 98312 | tf_op jit(solution)/shard_map/ppermute | solution.py:25
  88.7 8.6 %collective-permute-start.9 = (f32[16,1,4,128]{3,2,1,0:T(4,128)S(1)}, f32[16,1,4,128]{3,2,1,0:T(4,128)S(1)}, u32[]{:S(2)}, u32[]{:S(2)}) collective-permute-start(f32[16,1,4,128]{3,2,1,0:T(4,128)S(1)} %slice.618), channel_id=1, source_target_pairs={{0,4},{4,8},{8,12},{12,16},{16,20},{20,24},{24,28},{28,32},{32,36}... | collective-permute-start | bytes 98312 | tf_op jit(solution)/shard_map/ppermute | solution.py:37
  97.5 4.4 collective-permute-start.11
  99.5 8.6 %collective-permute-start.10 = (f32[16,1,4,128]{3,2,1,0:T(4,128)S(1)}, f32[16,1,4,128]{3,2,1,0:T(4,128)S(1)}, u32[]{:S(2)}, u32[]{:S(2)}) collective-permute-start(f32[16,1,4,128]{3,2,1,0:T(4,128)S(1)} %get-tuple-element.109), channel_id=1, source_target_pairs={{0,4},{4,8},{8,12},{12,16},{16,20},{20,24},{24,28},{28,32},{32,36}... | collective-permute-start | bytes 98312 | tf_op jit(solution)/shard_map/ppermute | solution.py:25
  108.5 4.4 collective-permute-start.13
  110.4 8.6 %collective-permute-start.12 = (f32[16,1,4,128]{3,2,1,0:T(4,128)S(1)}, f32[16,1,4,128]{3,2,1,0:T(4,128)S(1)}, u32[]{:S(2)}, u32[]{:S(2)}) collective-permute-start(f32[16,1,4,128]{3,2,1,0:T(4,128)S(1)} %get-tuple-element.101), channel_id=1, source_target_pairs={{0,4},{4,8},{8,12},{12,16},{16,20},{20,24},{24,28},{28,32},{32,36}... | collective-permute-start | bytes 98312 | tf_op jit(solution)/shard_map/ppermute | solution.py:25
  119.5 4.4 collective-permute-start.15
  121.4 8.6 %collective-permute-start.14 = (f32[16,1,4,128]{3,2,1,0:T(4,128)S(1)}, f32[16,1,4,128]{3,2,1,0:T(4,128)S(1)}, u32[]{:S(2)}, u32[]{:S(2)}) collective-permute-start(f32[16,1,4,128]{3,2,1,0:T(4,128)S(1)} %get-tuple-element.93), channel_id=1, source_target_pairs={{0,4},{4,8},{8,12},{12,16},{16,20},{20,24},{24,28},{28,32},{32,36}... | collective-permute-start | bytes 98312 | tf_op jit(solution)/shard_map/ppermute | solution.py:25
  130.2 3.5 collective-permute-start.16
  134.3 9.0 %collective-permute-start.18 = (f32[16,1,4,128]{3,2,1,0:T(4,128)S(1)}, f32[16,1,4,128]{3,2,1,0:T(4,128)S(1)}, u32[]{:S(2)}, u32[]{:S(2)}) collective-permute-start(f32[16,1,4,128]{3,2,1,0:T(4,128)S(1)} %get-tuple-element.70), channel_id=1, source_target_pairs={{4,0},{8,4},{12,8},{16,12},{20,16},{24,20},{28,24},{32,28},{36,32}... | collective-permute-start | bytes 98312 | tf_op jit(solution)/shard_map/ppermute | solution.py:27
  141.2 8.6 %collective-permute-start.17 = (f32[16,1,4,128]{3,2,1,0:T(4,128)S(1)}, f32[16,1,4,128]{3,2,1,0:T(4,128)S(1)}, u32[]{:S(2)}, u32[]{:S(2)}) collective-permute-start(f32[16,1,4,128]{3,2,1,0:T(4,128)S(1)} %get-tuple-element.69), channel_id=1, source_target_pairs={{0,4},{4,8},{8,12},{12,16},{16,20},{20,24},{24,28},{28,32},{32,36}... | collective-permute-start | bytes 98312 | tf_op jit(solution)/shard_map/ppermute | solution.py:25
  150.6 4.4 collective-permute-start.20
  152.5 8.6 %collective-permute-start.19 = (f32[16,1,4,128]{3,2,1,0:T(4,128)S(1)}, f32[16,1,4,128]{3,2,1,0:T(4,128)S(1)}, u32[]{:S(2)}, u32[]{:S(2)}) collective-permute-start(f32[16,1,4,128]{3,2,1,0:T(4,128)S(1)} %get-tuple-element.61), channel_id=1, source_target_pairs={{0,4},{4,8},{8,12},{12,16},{16,20},{20,24},{24,28},{28,32},{32,36}... | collective-permute-start | bytes 98312 | tf_op jit(solution)/shard_map/ppermute | solution.py:25
  161.5 3.5 collective-permute-start.21
  165.9 9.2 %collective-permute-start.23 = (f32[16,1,4,128]{3,2,1,0:T(4,128)S(1)}, f32[16,1,4,128]{3,2,1,0:T(4,128)S(1)}, u32[]{:S(2)}, u32[]{:S(2)}) collective-permute-start(f32[16,1,4,128]{3,2,1,0:T(4,128)S(1)} %get-tuple-element.38), channel_id=1, source_target_pairs={{4,0},{8,4},{12,8},{16,12},{20,16},{24,20},{28,24},{32,28},{36,32}... | collective-permute-start | bytes 98312 | tf_op jit(solution)/shard_map/ppermute | solution.py:27
  172.9 8.6 %collective-permute-start.22 = (f32[16,1,4,128]{3,2,1,0:T(4,128)S(1)}, f32[16,1,4,128]{3,2,1,0:T(4,128)S(1)}, u32[]{:S(2)}, u32[]{:S(2)}) collective-permute-start(f32[16,1,4,128]{3,2,1,0:T(4,128)S(1)} %get-tuple-element.37), channel_id=1, source_target_pairs={{0,4},{4,8},{8,12},{12,16},{16,20},{20,24},{24,28},{28,32},{32,36}... | collective-permute-start | bytes 98312 | tf_op jit(solution)/shard_map/ppermute | solution.py:25
  182.8 4.5 collective-permute-start.25
  184.7 8.6 %collective-permute-start.24 = (f32[16,1,4,128]{3,2,1,0:T(4,128)S(1)}, f32[16,1,4,128]{3,2,1,0:T(4,128)S(1)}, u32[]{:S(2)}, u32[]{:S(2)}) collective-permute-start(f32[16,1,4,128]{3,2,1,0:T(4,128)S(1)} %get-tuple-element.29), channel_id=1, source_target_pairs={{0,4},{4,8},{8,12},{12,16},{16,20},{20,24},{24,28},{28,32},{32,36}... | collective-permute-start | bytes 98312 | tf_op jit(solution)/shard_map/ppermute | solution.py:25
  194.1 26.6 %copy-start.1 = (f32[16,12,4,128]{3,2,1,0:T(4,128)}, f32[16,12,4,128]{3,2,1,0:T(4,128)S(1)}, u32[]{:S(2)}) copy-start(f32[16,12,4,128]{3,2,1,0:T(4,128)S(1)} %divide_add_fusion) | copy-start | bytes 1179652
  194.1 18.5 %collective-permute-start.30 = (f32[16,12,4,128]{3,2,1,0:T(4,128)S(1)}, f32[16,12,4,128]{3,2,1,0:T(4,128)S(1)}, u32[]{:S(2)}, u32[]{:S(2)}) collective-permute-start(f32[16,12,4,128]{3,2,1,0:T(4,128)S(1)} %divide_add_fusion), channel_id=1, source_target_pairs={{1,0},{2,1},{3,2},{0,3},{5,4},{6,5},{7,6},{4,7},{9,8},{10,9},{11,1... | collective-permute-start | bytes 1179656 | tf_op jit(solution)/shard_map/ppermute | solution.py:126
  198.8 10.9 %collective-permute-start.28 = (f32[16,12,4,128]{3,2,1,0:T(4,128)S(1)}, f32[16,12,4,128]{3,2,1,0:T(4,128)S(1)}, u32[]{:S(2)}, u32[]{:S(2)}) collective-permute-start(f32[16,12,4,128]{3,2,1,0:T(4,128)S(1)} %divide_add_fusion), channel_id=1, source_target_pairs={{0,1},{1,2},{2,3},{3,0},{4,5},{5,6},{6,7},{7,4},{8,9},{9,10},{10,1... | collective-permute-start | bytes 1179656 | tf_op jit(solution)/shard_map/ppermute | solution.py:124
  200.7 11.0 %collective-permute-start.27 = (f32[16,1,4,128]{3,2,1,0:T(4,128)S(1)}, f32[16,1,4,128]{3,2,1,0:T(4,128)S(1)}, u32[]{:S(2)}, u32[]{:S(2)}) collective-permute-start(f32[16,1,4,128]{3,2,1,0:T(4,128)S(1)} %get-tuple-element.22), channel_id=1, source_target_pairs={{4,0},{8,4},{12,8},{16,12},{20,16},{24,20},{28,24},{32,28},{36,32}... | collective-permute-start | bytes 98312 | tf_op jit(solution)/shard_map/ppermute | solution.py:27
  202.7 9.1 %collective-permute-start.26 = (f32[16,1,4,128]{3,2,1,0:T(4,128)S(1)}, f32[16,1,4,128]{3,2,1,0:T(4,128)S(1)}, u32[]{:S(2)}, u32[]{:S(2)}) collective-permute-start(f32[16,1,4,128]{3,2,1,0:T(4,128)S(1)} %get-tuple-element.21), channel_id=1, source_target_pairs={{0,4},{4,8},{8,12},{12,16},{16,20},{20,24},{24,28},{28,32},{32,36}... | collective-permute-start | bytes 98312 | tf_op jit(solution)/shard_map/ppermute | solution.py:25
  209.7 2.8 copy-start.2
  209.7 11.0 %collective-permute-start.29 = (f32[16,12,4,128]{3,2,1,0:T(4,128)S(1)}, f32[16,12,4,128]{3,2,1,0:T(4,128)}, u32[]{:S(2)}, u32[]{:S(2)}) collective-permute-start(f32[16,12,4,128]{3,2,1,0:T(4,128)S(1)} %collective-permute-done.28), channel_id=1, source_target_pairs={{0,1},{1,2},{2,3},{3,0},{4,5},{5,6},{6,7},{7,4},{8,9},{9,10},{10,1... | collective-permute-start | bytes 1179656 | tf_op jit(solution)/shard_map/ppermute | solution.py:124
